TPU v7x, 32 devices: a whole 2x2x4 slice. The times are simulated.
32 devices in a mesh: energy: 8 (over y, x, core), elem: 4 (over z).
Axes of the slice: x: 2, y: 2, z: 4, core: 2. Of those that a mesh axis runs over, the one named last changes fastest.
Arguments:
- g_lesser: bfloat16 [2, 512, 2048], P(None, 'energy', 'elem'), may hold values from -6 to 6
- g_greater: bfloat16 [2, 512, 2048], P(None, 'energy', 'elem'), may hold values from -6 to 6
- send_rows: int32 [4, 8, 4, 32], P('elem'), may hold values from 0 to 63, as said below
- partner_slot: int32 [2048], P('elem'), may hold values from 0 to 127, as said below
Outputs:
- polarization_lesser: bfloat16 [2, 512, 2048], P(None, 'energy', 'elem')
- polarization_greater: bfloat16 [2, 512, 2048], P(None, 'energy', 'elem')
Inputs may be any that keep to these rules, and one draw needn't show every extreme that they name: partner is an involution on the elements that keeps the element piece n. The groups fall into two halves of 2 groups; for a sending group b and element piece n, send_rows[b, n, a, :] lists 32 distinct rows when a lies in b's half (b itself included) and zeros otherwise; every row of that piece of the sender appears exactly once over all receivers of its half. `partner_slot`: every slot named points into a receiving group's half and to a slot that carries a row; the 64 elements of one element piece of a group name 64 distinct slots.
All inputs are finite; a program needn't handle non-finite values.
Results may differ from a plain program's by a relative error of at most 0.001.
Values may be sent and summed in bfloat16 or wider, within the bound.
No kernel may reach another device: no remote copies, remote signals or barrier semaphores. Data moves between devices by JAX's collectives and lax.ppermute only.
A program may use at most 64 MiB of HBM per device.

v0:
```python
from functools import partial
import math
import jax
import jax.numpy as jnp
from jax import lax
from jax.sharding import PartitionSpec as P


def factor_pair(length):
    divisor = math.isqrt(length)
    while length % divisor:
        divisor -= 1
    return divisor


def phase_tables(rows_count, cols_count, modulus, inverse):
    sign_factor = 1.0 if inverse else -1.0
    left_index = jnp.arange(rows_count, dtype=jnp.int32)
    right_index = jnp.arange(cols_count, dtype=jnp.int32)
    phases = (left_index[:, None] * right_index[None, :] % modulus).astype(jnp.float32) * (
        2.0 * math.pi / modulus
    )
    return (jnp.cos(phases), sign_factor * jnp.sin(phases))


def transform(real_part, imag_part, inverse):
    signals, length, width = real_part.shape
    first_size = factor_pair(length)
    second_size = length // first_size
    cos_first, sin_first = phase_tables(first_size, first_size, first_size, inverse)
    cos_twist, sin_twist = phase_tables(first_size, second_size, length, inverse)
    cos_second, sin_second = phase_tables(second_size, second_size, second_size, inverse)
    product = partial(jnp.einsum, precision=lax.Precision.HIGHEST)
    real_grid = real_part.reshape(signals, first_size, second_size, width)
    imag_grid = imag_part.reshape(signals, first_size, second_size, width)
    inner_re = product("ka,sabe->skbe", cos_first, real_grid) - product(
        "ka,sabe->skbe", sin_first, imag_grid
    )
    inner_im = product("ka,sabe->skbe", cos_first, imag_grid) + product(
        "ka,sabe->skbe", sin_first, real_grid
    )
    twist_cos = cos_twist[None, :, :, None]
    twist_sin = sin_twist[None, :, :, None]
    twist_re = inner_re * twist_cos - inner_im * twist_sin
    twist_im = inner_re * twist_sin + inner_im * twist_cos
    outer_re = product("qb,skbe->sqke", cos_second, twist_re) - product(
        "qb,skbe->sqke", sin_second, twist_im
    )
    outer_im = product("qb,skbe->sqke", cos_second, twist_im) + product(
        "qb,skbe->sqke", sin_second, twist_re
    )
    return (outer_re.reshape(signals, length, width), outer_im.reshape(signals, length, width))


def reverse_energy(values):
    return jnp.roll(jnp.flip(values, axis=1), 1, axis=1)


def shards(g_lesser, g_greater, send_rows, partner_slot):
    piece_index = lax.axis_index("energy")
    energy_count = lax.axis_size("energy")
    group_rows = partner_slot.shape[0]
    elem_dev = group_rows // energy_count
    own_lesser, own_greater = (
        lax.all_to_all(g_lesser, "energy", split_axis=2, concat_axis=1, tiled=True),
        lax.all_to_all(g_greater, "energy", split_axis=2, concat_axis=1, tiled=True),
    )
    own_rows = jnp.stack([own_lesser, own_greater])
    partner_columns = lax.dynamic_slice_in_dim(partner_slot, piece_index * elem_dev, elem_dev, 0)
    chosen_rows = lax.dynamic_index_in_dim(send_rows[0], piece_index, 0, keepdims=False).reshape(-1)
    outgoing = jnp.take(own_rows, chosen_rows, axis=3)
    incoming = lax.all_to_all(outgoing, "elem", split_axis=3, concat_axis=3, tiled=True)
    partner_rows = jnp.take(incoming, partner_columns, axis=3)
    signals = jnp.concatenate([own_rows, partner_rows], 0).astype(jnp.float32)
    spec_re, spec_im = transform(signals[:, 0], signals[:, 1], False)
    near_re = spec_re[:2]
    near_im = spec_im[:2]
    far_re = reverse_energy(jnp.stack([spec_re[3], spec_re[2]]))
    far_im = reverse_energy(jnp.stack([spec_im[3], spec_im[2]]))
    prod_re = near_re * far_re - near_im * far_im
    prod_im = near_re * far_im + near_im * far_re
    back_re, back_im = transform(prod_re, prod_im, True)
    length = back_re.shape[1]
    factor = 1.0 / (length * math.sqrt(length))
    result = jnp.stack([factor * back_im, -factor * back_re], 1).astype(jnp.bfloat16)
    lesser_out, greater_out = (
        lax.all_to_all(result[0], "energy", split_axis=1, concat_axis=2, tiled=True),
        lax.all_to_all(result[1], "energy", split_axis=1, concat_axis=2, tiled=True),
    )
    return (lesser_out, greater_out)


def solution(mesh):
    in_specs = (
        P(None, "energy", "elem"),
        P(None, "energy", "elem"),
        P("elem", None, None, None),
        P("elem"),
    )
    out_specs = (P(None, "energy", "elem"), P(None, "energy", "elem"))
    return jax.shard_map(shards, mesh=mesh, in_specs=in_specs, out_specs=out_specs, check_vma=False)
```

profile of v0, /device:TPU:0, one launch (start us, length us, event | category | flops | bytes accessed | tf_op | source)
XLA Modules:
  0.0 93.1 jit_solution(4972418240594326676)
XLA Ops:
  0.6 1.1 %copy.86 = bf16[2,64,512]{1,0,2:T(2,128)(2,1)S(1)} copy(bf16[2,64,512]{2,1,0:T(8,128)(2,1)} %param.4) | data formatting | bytes 262144 | tf_op args[0]
  1.7 0.9 reshape.175
  2.6 5.3 %all-to-all-start = ((bf16[8,2,4096]{2,1,0:T(2,128)(2,1)}), bf16[8,2,4096]{2,1,0:T(2,128)(2,1)S(1)}, u32[]{:S(2)}, u32[]{:S(2)}) async-start(bf16[8,2,4096]{2,1,0:T(2,128)(2,1)} %reshape.175), calls=%async_computation | async-start | bytes 262144 | tf_op jit(solution)/shard_map/all_to_all | solution.py:65
  8.3 0.9 reshape.173
  9.2 4.3 %all-to-all-done = bf16[8,2,4096]{2,1,0:T(2,128)(2,1)S(1)} async-done(((bf16[8,2,4096]{2,1,0:T(2,128)(2,1)}), bf16[8,2,4096]{2,1,0:T(2,128)(2,1)S(1)}, u32[]{:S(2)}, u32[]{:S(2)}) %all-to-all-start) | async-done | bytes 131104 | tf_op jit(solution)/shard_map/all_to_all | solution.py:65
  13.5 3.4 %all-to-all-start.1 = ((bf16[8,2,4096]{2,1,0:T(2,128)(2,1)}), bf16[8,2,4096]{2,1,0:T(2,128)(2,1)S(1)}, u32[]{:S(2)}, u32[]{:S(2)}) async-start(bf16[8,2,4096]{2,1,0:T(2,128)(2,1)} %reshape.173), calls=%async_computation.1 | async-start | bytes 262144 | tf_op jit(solution)/shard_map/all_to_all | solution.py:66
  17.6 4.7 %all-to-all-done.1 = bf16[8,2,4096]{2,1,0:T(2,128)(2,1)S(1)} async-done(((bf16[8,2,4096]{2,1,0:T(2,128)(2,1)}), bf16[8,2,4096]{2,1,0:T(2,128)(2,1)S(1)}, u32[]{:S(2)}, u32[]{:S(2)}) %all-to-all-start.1) | async-done | bytes 131104 | tf_op jit(solution)/shard_map/all_to_all | solution.py:66
  23.1 0.4 pad_maximum_fusion.4
  23.4 1.7 %gather_fusion = bf16[128,2,2,512]{3,2,1,0:T(2,128)(2,1)S(1)} fusion(bf16[2,2,512,64]{2,1,3,0:T(2,128)(2,1)S(1)} %pad_maximum_fusion.4, s32[1024]{0:T(1024)S(1)} %pad_clamp_fusion.1), kind=kCustom, calls=%fused_computation | custom fusion | bytes 1049088 | tf_op jit(solution)/shard_map/jit(_take)/gather | solution.py:71
  25.1 1.4 %fusion.22 = bf16[2,2,512,128]{2,1,0,3:T(2,128)(2,1)} fusion(bf16[128,2,2,512]{3,2,1,0:T(2,128)(2,1)S(1)} %gather_fusion, pred[128]{0:T(512)(128)(4,1)S(1)} %compare_and_fusion), kind=kLoop, calls=%fused_computation.49 | loop fusion | flops 262144 | bytes 1048704 | tf_op jit(solution)/shard_map/jit(_take)/select_n | solution.py:71
  26.5 4.9 %all-to-all-start.2 = ((bf16[2,2,512,128]{2,1,0,3:T(2,128)(2,1)}), bf16[2,2,512,128]{2,1,0,3:T(2,128)(2,1)S(1)}, u32[]{:S(2)}, u32[]{:S(2)}) async-start(bf16[2,2,512,128]{2,1,0,3:T(2,128)(2,1)} %fusion.22), calls=%async_computation.2 | async-start | bytes 1048576 | tf_op jit(solution)/shard_map/all_to_all | solution.py:72
  31.4 0.8 compare_and_fusion.1
  32.6 13.1 %all-to-all-done.2 = bf16[2,2,512,128]{2,1,0,3:T(2,128)(2,1)S(1)} async-done(((bf16[2,2,512,128]{2,1,0,3:T(2,128)(2,1)}), bf16[2,2,512,128]{2,1,0,3:T(2,128)(2,1)S(1)}, u32[]{:S(2)}, u32[]{:S(2)}) %all-to-all-start.2) | async-done | bytes 524320 | tf_op jit(solution)/shard_map/all_to_all | solution.py:72
  46.0 1.1 %gather_fusion.1 = bf16[64,2,2,512]{3,2,1,0:T(2,128)(2,1)S(1)} fusion(bf16[2,2,512,128]{2,1,3,0:T(2,128)(2,1)S(1)} %copy.92, s32[1024]{0:T(1024)S(1)} %pad_clamp_fusion), kind=kCustom, calls=%fused_computation.1 | custom fusion | bytes 524544 | tf_op jit(solution)/shard_map/jit(_take)/gather | solution.py:73
  47.5 0.7 pad_maximum_fusion.2
  48.2 0.7 fusion.180
  48.9 0.5 copy.95
  49.5 0.7 copy.97
  50.2 0.6 fusion.35
  50.8 0.6 fusion.39
  51.4 0.6 fusion.3
  52.1 0.9 multiply_add_fusion
  53.0 1.4 %fusion.12 = f32[4,16,64,32]{2,3,1,0:T(8,128)S(1)} fusion(f32[4,16,32,64]{3,1,2,0:T(8,128)S(1)} %get-tuple-element.4), kind=kOutput, calls=%fused_computation.25 | convolution fusion | flops 50345984 | bytes 1048576 | tf_op jit(solution)/shard_map/qb,skbe->sqke/dot_general | solution.py:49
  54.4 1.4 %fusion.16 = f32[4,16,64,32]{2,3,1,0:T(8,128)S(1)} fusion(f32[4,16,32,64]{3,1,2,0:T(8,128)S(1)} %get-tuple-element.5), kind=kOutput, calls=%fused_computation.29 | convolution fusion | flops 50345984 | bytes 1048576 | tf_op jit(solution)/shard_map/qb,skbe->sqke/dot_general | solution.py:46
  55.8 1.4 %fusion.1 = f32[4,32,16,64]{3,1,2,0:T(8,128)S(1)} fusion(f32[4,16,64,32]{2,3,1,0:T(8,128)S(1)} %fusion.16, f32[4,16,32,64]{3,1,2,0:T(8,128)S(1)} %get-tuple-element.4), kind=kOutput, calls=%fused_computation.5 | convolution fusion | flops 50478080 | bytes 1572864 | tf_op jit(solution)/shard_map/qb,skbe->sqke/dot_general | solution.py:46
  57.2 1.0 %copy-done.1 = f32[4,32,16,64]{3,1,2,0:T(8,128)} copy-done((f32[4,32,16,64]{3,1,2,0:T(8,128)}, f32[4,32,16,64]{3,1,2,0:T(8,128)S(1)}, u32[]{:S(2)}) %copy-start.1) | copy-done | bytes 524312
  58.2 1.4 %fusion = f32[4,32,16,64]{3,1,2,0:T(8,128)S(1)} fusion(f32[4,16,64,32]{2,3,1,0:T(8,128)S(1)} %fusion.12, f32[4,16,32,64]{3,1,2,0:T(8,128)S(1)} %get-tuple-element.5), kind=kOutput, calls=%fused_computation.3 | convolution fusion | flops 50478080 | bytes 1572864 | tf_op jit(solution)/shard_map/qb,skbe->sqke/dot_general | solution.py:49
  59.6 1.0 %copy-done.2 = f32[4,32,16,64]{3,1,2,0:T(8,128)} copy-done((f32[4,32,16,64]{3,1,2,0:T(8,128)}, f32[4,32,16,64]{3,1,2,0:T(8,128)S(1)}, u32[]{:S(2)}) %copy-start.2) | copy-done | bytes 524312
  60.8 0.9 slice-done
  62.2 0.7 slice.80
  63.1 0.9 slice-done.1
  64.5 0.9 slice.89
  65.7 0.9 fusion.33
  66.6 0.9 fusion.29
  67.5 0.9 fusion.7
  68.4 1.1 %multiply_subtract_fusion.1 = (f32[2,16,32,64]{3,1,2,0:T(8,128)S(1)}, f32[2,16,32,64]{3,1,2,0:T(8,128)S(1)}) fusion(f32[2,16,32,64]{3,1,2,0:T(8,128)S(1)} %fusion.7, f32[16,32]{0,1:T(8,128)S(1)} %get-tuple-element.19, f32[16,32]{0,1:T(8,128)S(1)} %fusion.90, f32[2,32,64,16]{2,3,1,0:T(8,128)S(1)} %fusion.29, f32[2,16,32,64]{3,2,1,0:T(8,128)S(1)} %get-tuple-element.6), kind=kOutput, calls=%fused_computation.47 | convolution fusion | flops 13045248 | bytes 1314816 | tf_op jit(solution)/shard_map/ka,sabe->skbe/dot_general | solution.py:39
  69.5 0.8 fusion.23
  70.3 0.8 fusion.27
  71.0 0.8 fusion.10
  71.8 0.8 fusion.11
  73.2 0.9 reshape.179
  74.1 3.4 %all-to-all-start.4 = ((bf16[8,2,4096]{2,1,0:T(2,128)(2,1)}), bf16[8,2,4096]{2,1,0:T(2,128)(2,1)S(1)}, u32[]{:S(2)}, u32[]{:S(2)}) async-start(bf16[8,2,4096]{2,1,0:T(2,128)(2,1)} %reshape.179), calls=%async_computation.4 | async-start | bytes 262144 | tf_op jit(solution)/shard_map/all_to_all | solution.py:88
  77.8 0.9 reshape.177
  78.7 4.3 %all-to-all-done.4 = bf16[8,2,4096]{2,1,0:T(2,128)(2,1)S(1)} async-done(((bf16[8,2,4096]{2,1,0:T(2,128)(2,1)}), bf16[8,2,4096]{2,1,0:T(2,128)(2,1)S(1)}, u32[]{:S(2)}, u32[]{:S(2)}) %all-to-all-start.4) | async-done | bytes 131104 | tf_op jit(solution)/shard_map/all_to_all | solution.py:88
  83.0 3.4 %all-to-all-start.3 = ((bf16[8,2,4096]{2,1,0:T(2,128)(2,1)}), bf16[8,2,4096]{2,1,0:T(2,128)(2,1)S(1)}, u32[]{:S(2)}, u32[]{:S(2)}) async-start(bf16[8,2,4096]{2,1,0:T(2,128)(2,1)} %reshape.177), calls=%async_computation.3 | async-start | bytes 262144 | tf_op jit(solution)/shard_map/all_to_all | solution.py:87
  86.8 0.9 all_to_all.65
  87.6 4.2 %all-to-all-done.3 = bf16[8,2,4096]{2,1,0:T(2,128)(2,1)S(1)} async-done(((bf16[8,2,4096]{2,1,0:T(2,128)(2,1)}), bf16[8,2,4096]{2,1,0:T(2,128)(2,1)S(1)}, u32[]{:S(2)}, u32[]{:S(2)}) %all-to-all-start.3) | async-done | bytes 131104 | tf_op jit(solution)/shard_map/all_to_all | solution.py:87
  92.2 0.9 all_to_all.61
  (52 shorter events, 6.4 us)
Async XLA Ops:
  0.6 7.3 %copy-start = (s32[1,8,4,32]{3,2,1,0:T(4,128)S(1)}, s32[1,8,4,32]{3,2,1,0:T(4,128)}, u32[]{:S(2)}) copy-start(s32[1,8,4,32]{3,2,1,0:T(4,128)} %param.6) | copy-start | bytes 12292
  2.6 5.5 %copy-start.3 = (bf16[2,64,512]{2,1,0:T(8,128)(2,1)S(1)}, bf16[2,64,512]{2,1,0:T(8,128)(2,1)}, u32[]{:S(2)}) copy-start(bf16[2,64,512]{2,1,0:T(8,128)(2,1)} %param.5) | copy-start | bytes 393220
  2.6 10.8 %all-to-all-start = ((bf16[8,2,4096]{2,1,0:T(2,128)(2,1)}), bf16[8,2,4096]{2,1,0:T(2,128)(2,1)S(1)}, u32[]{:S(2)}, u32[]{:S(2)}) async-start(bf16[8,2,4096]{2,1,0:T(2,128)(2,1)} %reshape.175), calls=%async_computation | async-start | bytes 262144 | tf_op jit(solution)/shard_map/all_to_all | solution.py:65
  13.5 8.8 %all-to-all-start.1 = ((bf16[8,2,4096]{2,1,0:T(2,128)(2,1)}), bf16[8,2,4096]{2,1,0:T(2,128)(2,1)S(1)}, u32[]{:S(2)}, u32[]{:S(2)}) async-start(bf16[8,2,4096]{2,1,0:T(2,128)(2,1)} %reshape.173), calls=%async_computation.1 | async-start | bytes 262144 | tf_op jit(solution)/shard_map/all_to_all | solution.py:66
  26.5 19.2 %all-to-all-start.2 = ((bf16[2,2,512,128]{2,1,0,3:T(2,128)(2,1)}), bf16[2,2,512,128]{2,1,0,3:T(2,128)(2,1)S(1)}, u32[]{:S(2)}, u32[]{:S(2)}) async-start(bf16[2,2,512,128]{2,1,0,3:T(2,128)(2,1)} %fusion.22), calls=%async_computation.2 | async-start | bytes 1048576 | tf_op jit(solution)/shard_map/all_to_all | solution.py:72
  57.2 1.0 %copy-start.1 = (f32[4,32,16,64]{3,1,2,0:T(8,128)}, f32[4,32,16,64]{3,1,2,0:T(8,128)S(1)}, u32[]{:S(2)}) copy-start(f32[4,32,16,64]{3,1,2,0:T(8,128)S(1)} %fusion.1) | copy-start | bytes 1572868
  59.6 1.0 %copy-start.2 = (f32[4,32,16,64]{3,1,2,0:T(8,128)}, f32[4,32,16,64]{3,1,2,0:T(8,128)S(1)}, u32[]{:S(2)}) copy-start(f32[4,32,16,64]{3,1,2,0:T(8,128)S(1)} %fusion) | copy-start | bytes 1572868
  60.6 1.0 %slice-start = ((f32[4,32,16,64]{3,1,2,0:T(8,128)}), f32[2,32,16,64]{3,1,2,0:T(8,128)S(1)}, s32[]{:S(2)}) async-start(f32[4,32,16,64]{3,1,2,0:T(8,128)} %copy-done.1), calls=%async_computation.5 | async-start | bytes 1048576 | tf_op jit(solution)/shard_map/slice | solution.py:76
  62.9 1.0 %slice-start.1 = ((f32[4,32,16,64]{3,1,2,0:T(8,128)}), f32[2,32,16,64]{3,1,2,0:T(8,128)S(1)}, s32[]{:S(2)}) async-start(f32[4,32,16,64]{3,1,2,0:T(8,128)} %copy-done.2), calls=%async_computation.6 | async-start | bytes 1048576 | tf_op jit(solution)/shard_map/slice | solution.py:77
  74.1 8.8 %all-to-all-start.4 = ((bf16[8,2,4096]{2,1,0:T(2,128)(2,1)}), bf16[8,2,4096]{2,1,0:T(2,128)(2,1)S(1)}, u32[]{:S(2)}, u32[]{:S(2)}) async-start(bf16[8,2,4096]{2,1,0:T(2,128)(2,1)} %reshape.179), calls=%async_computation.4 | async-start | bytes 262144 | tf_op jit(solution)/shard_map/all_to_all | solution.py:88
  83.0 8.8 %all-to-all-start.3 = ((bf16[8,2,4096]{2,1,0:T(2,128)(2,1)}), bf16[8,2,4096]{2,1,0:T(2,128)(2,1)S(1)}, u32[]{:S(2)}, u32[]{:S(2)}) async-start(bf16[8,2,4096]{2,1,0:T(2,128)(2,1)} %reshape.177), calls=%async_computation.3 | async-start | bytes 262144 | tf_op jit(solution)/shard_map/all_to_all | solution.py:87
where the time goes:
time: 93.8 us; the launch traced here: 93.1 us
  waiting for transfers between devices  30.5 us (33%)
  local copies, waits for them, and re-layouts  21.7 us (23%)
  starting transfers between devices  20.3 us (22%)
  matrix products  15.2 us (16%)
  other arithmetic  4.33 us (5%)
  between operations  1.15 us (1%)
    all_to_all x1, waiting for transfers between devices, shards(): lax.all_to_all(outgoing, 'elem', split_axis=3, concat_axis=3, tiled=True)  13.1 us
    unnamed x18, local copies, waits for them, and re-layouts  7.64 us
    all_to_all x1, starting transfers between devices, shards(): lax.all_to_all(g_lesser, 'energy', split_axis=2, concat_axis=1, tiled=True)  5.3 us
    all_to_all x1, starting transfers between devices, shards(): lax.all_to_all(outgoing, 'elem', split_axis=3, concat_axis=3, tiled=True)  4.87 us
    all_to_all x1, waiting for transfers between devices, shards(): lax.all_to_all(g_greater, 'energy', split_axis=2, concat_axis=1, tiled=True)  4.68 us
    all_to_all x1, waiting for transfers between devices, shards(): lax.all_to_all(result[1], 'energy', split_axis=1, concat_axis=2, tiled=True)  4.29 us
    all_to_all x1, waiting for transfers between devices, shards(): lax.all_to_all(g_lesser, 'energy', split_axis=2, concat_axis=1, tiled=True)  4.26 us
    all_to_all x1, waiting for transfers between devices, shards(): lax.all_to_all(result[0], 'energy', split_axis=1, concat_axis=2, tiled=True)  4.19 us
  transfers between devices with their start and end apart: 5, of which 5 were waited for; matrix products, arithmetic and copies ran while one was open for 5% of the time, Pallas kernels for 0%

commit v1 on v0

--- a/solution.py
+++ b/solution.py
@@ -4,6 +4,22 @@
 import jax.numpy as jnp
 from jax import lax
 from jax.sharding import PartitionSpec as P
+
+
+def swapped_with_each(x, axis, split, join):
+    ways, here = (lax.axis_size(axis), lax.axis_index(axis))
+    width = x.shape[split] // ways
+    dims = list(x.shape)
+    dims[split] = width
+    height = dims[join]
+    dims[join] = height * ways
+    full = jnp.zeros(dims, x.dtype)
+    for mask in range(ways):
+        part = lax.dynamic_slice_in_dim(x, (here ^ mask) * width, width, axis=split)
+        if mask:
+            part = lax.ppermute(part, axis, [(d, d ^ mask) for d in range(ways)])
+        full = lax.dynamic_update_slice_in_dim(full, part, (here ^ mask) * height, axis=join)
+    return full
 
 
 def factor_pair(length):
@@ -69,7 +85,7 @@
     partner_columns = lax.dynamic_slice_in_dim(partner_slot, piece_index * elem_dev, elem_dev, 0)
     chosen_rows = lax.dynamic_index_in_dim(send_rows[0], piece_index, 0, keepdims=False).reshape(-1)
     outgoing = jnp.take(own_rows, chosen_rows, axis=3)
-    incoming = lax.all_to_all(outgoing, "elem", split_axis=3, concat_axis=3, tiled=True)
+    incoming = swapped_with_each(outgoing, "elem", 3, 3)
     partner_rows = jnp.take(incoming, partner_columns, axis=3)
     signals = jnp.concatenate([own_rows, partner_rows], 0).astype(jnp.float32)
     spec_re, spec_im = transform(signals[:, 0], signals[:, 1], False)

time: 93.8 us -> 88.7 us (0.946)
  waiting for transfers between devices: 30.5 us -> 25.9 us
    all_to_all x1 -> x0, waiting for transfers between devices: 13.1 us -> none  [shards(): lax.all_to_all(outgoing, 'elem', split_axis=3, concat_axis=3, tiled=True)]
    ppermute x0 -> x3, waiting for transfers between devices: none -> 9.59 us  [swapped_with_each(): part = lax.ppermute(part, axis, [(d, d ^ mask) for d in range(ways)])]
    all_to_all x1 -> x0, starting transfers between devices: 4.87 us -> none  [shards(): lax.all_to_all(outgoing, 'elem', split_axis=3, concat_axis=3, tiled=True)]
    ppermute x0 -> x3, starting transfers between devices: none -> 4.45 us  [swapped_with_each(): part = lax.ppermute(part, axis, [(d, d ^ mask) for d in range(ways)])]
  transfers between devices with their start and end apart: 5 -> 7, of which waited for: 5 -> 6; matrix products, arithmetic and copies ran while one was open for 5% -> 6% of each run, Pallas kernels for 0% -> 0%
where the time goes in v1:
time: 88.7 us; the launch traced here: 88.1 us
  waiting for transfers between devices  25.9 us (29%)
  local copies, waits for them, and re-layouts  22.4 us (25%)
  starting transfers between devices  19.9 us (22%)
  matrix products  15.2 us (17%)
  other arithmetic  3.55 us (4%)
  between operations  1.2 us (1%)
    ppermute x3, waiting for transfers between devices, swapped_with_each(): part = lax.ppermute(part, axis, [(d, d ^ mask) for d in range(ways)])  9.59 us
    unnamed x18, local copies, waits for them, and re-layouts  7.63 us
    all_to_all x1, starting transfers between devices, shards(): lax.all_to_all(g_lesser, 'energy', split_axis=2, concat_axis=1, tiled=True)  5.3 us
    ppermute x3, starting transfers between devices, swapped_with_each(): part = lax.ppermute(part, axis, [(d, d ^ mask) for d in range(ways)])  4.45 us
    all_to_all x1, waiting for transfers between devices, shards(): lax.all_to_all(g_greater, 'energy', split_axis=2, concat_axis=1, tiled=True)  4.44 us
    all_to_all x1, waiting for transfers between devices, shards(): lax.all_to_all(result[1], 'energy', split_axis=1, concat_axis=2, tiled=True)  4.29 us
    all_to_all x1, waiting for transfers between devices, shards(): lax.all_to_all(result[0], 'energy', split_axis=1, concat_axis=2, tiled=True)  4.19 us
    all_to_all x1, waiting for transfers between devices, shards(): lax.all_to_all(g_lesser, 'energy', split_axis=2, concat_axis=1, tiled=True)  3.39 us
  transfers between devices with their start and end apart: 7, of which 6 were waited for; matrix products, arithmetic and copies ran while one was open for 6% of the time, Pallas kernels for 0%

profile of v1, /device:TPU:0, one launch (start us, length us, event | category | flops | bytes accessed | tf_op | source)
XLA Modules:
  0.0 88.1 jit_solution(11316423350344994223)
XLA Ops:
  0.6 1.1 %copy.92 = bf16[2,64,512]{1,0,2:T(2,128)(2,1)S(1)} copy(bf16[2,64,512]{2,1,0:T(8,128)(2,1)} %param.4) | data formatting | bytes 262144 | tf_op args[0]
  1.7 0.9 %reshape.175 = bf16[8,2,4096]{2,1,0:T(2,128)(2,1)} reshape(bf16[512,2,64]{2,1,0:T(2,128)(2,1)S(1)} %bitcast.170) | data formatting | bytes 262144
  2.6 5.3 %all-to-all-start = ((bf16[8,2,4096]{2,1,0:T(2,128)(2,1)}), bf16[8,2,4096]{2,1,0:T(2,128)(2,1)S(1)}, u32[]{:S(2)}, u32[]{:S(2)}) async-start(bf16[8,2,4096]{2,1,0:T(2,128)(2,1)} %reshape.175), calls=%async_computation | async-start | bytes 262144 | tf_op jit(solution)/shard_map/all_to_all | solution.py:81
  8.1 0.8 compare_and_fusion.1
  9.1 0.9 %reshape.173 = bf16[8,2,4096]{2,1,0:T(2,128)(2,1)} reshape(bf16[512,2,64]{2,1,0:T(2,128)(2,1)S(1)} %bitcast.171) | data formatting | bytes 262144
  10.1 3.4 %all-to-all-done = bf16[8,2,4096]{2,1,0:T(2,128)(2,1)S(1)} async-done(((bf16[8,2,4096]{2,1,0:T(2,128)(2,1)}), bf16[8,2,4096]{2,1,0:T(2,128)(2,1)S(1)}, u32[]{:S(2)}, u32[]{:S(2)}) %all-to-all-start) | async-done | bytes 131104 | tf_op jit(solution)/shard_map/all_to_all | solution.py:81
  13.5 3.4 %all-to-all-start.1 = ((bf16[8,2,4096]{2,1,0:T(2,128)(2,1)}), bf16[8,2,4096]{2,1,0:T(2,128)(2,1)S(1)}, u32[]{:S(2)}, u32[]{:S(2)}) async-start(bf16[8,2,4096]{2,1,0:T(2,128)(2,1)} %reshape.173), calls=%async_computation.1 | async-start | bytes 262144 | tf_op jit(solution)/shard_map/all_to_all | solution.py:82
  17.9 4.4 %all-to-all-done.1 = bf16[8,2,4096]{2,1,0:T(2,128)(2,1)S(1)} async-done(((bf16[8,2,4096]{2,1,0:T(2,128)(2,1)}), bf16[8,2,4096]{2,1,0:T(2,128)(2,1)S(1)}, u32[]{:S(2)}, u32[]{:S(2)}) %all-to-all-start.1) | async-done | bytes 131104 | tf_op jit(solution)/shard_map/all_to_all | solution.py:82
  23.6 1.7 %gather_fusion = bf16[128,2,2,512]{3,2,1,0:T(2,128)(2,1)S(1)} fusion(bf16[2,2,512,64]{2,1,3,0:T(2,128)(2,1)S(1)} %pad_maximum_fusion.4, s32[1024]{0:T(1024)S(1)} %pad_clamp_fusion.1), kind=kCustom, calls=%fused_computation | custom fusion | bytes 1049088 | tf_op jit(solution)/shard_map/jit(_take)/gather | solution.py:87
  25.3 0.6 broadcast_select_fusion
  26.2 3.7 %collective-permute-start.2 = (bf16[2,2,512,32]{2,1,0,3:T(2,128)(2,1)S(1)}, bf16[2,2,512,32]{2,1,0,3:T(2,128)(2,1)S(1)}, u32[]{:S(2)}, u32[]{:S(2)}) collective-permute-start(bf16[2,2,512,32]{2,1,0,3:T(2,128)(2,1)S(1)} %get-tuple-element.18), channel_id=1, source_target_pairs={{0,3},{1,2},{2,1},{3,0},{4,7},{5,6},{6,5},{7,4},{8,11},{9,10},{10,... | collective-permute-start | bytes 393224 | tf_op jit(solution)/shard_map/ppermute | solution.py:20
  29.9 0.8 collective-permute-start
  31.1 7.0 %collective-permute-done = bf16[2,2,512,32]{2,1,0,3:T(2,128)(2,1)S(1)} collective-permute-done((bf16[2,2,512,32]{2,1,0,3:T(2,128)(2,1)S(1)}, bf16[2,2,512,32]{2,1,0,3:T(2,128)(2,1)S(1)}, u32[]{:S(2)}, u32[]{:S(2)}) %collective-permute-start) | collective-permute-done | bytes 131104 | tf_op jit(solution)/shard_map/ppermute | solution.py:20
  38.2 2.5 %collective-permute-done.1 = bf16[2,2,512,32]{2,1,0,3:T(2,128)(2,1)S(1)} collective-permute-done((bf16[2,2,512,32]{2,1,0,3:T(2,128)(2,1)S(1)}, bf16[2,2,512,32]{2,1,0,3:T(2,128)(2,1)S(1)}, u32[]{:S(2)}, u32[]{:S(2)}) %collective-permute-start.1) | collective-permute-done | bytes 131104 | tf_op jit(solution)/shard_map/ppermute | solution.py:20
  41.0 1.1 %gather_fusion.1 = bf16[64,2,2,512]{3,2,1,0:T(2,128)(2,1)S(1)} fusion(bf16[2,2,512,128]{2,1,3,0:T(2,128)(2,1)S(1)} %copy_dynamic-update-slice_fusion, s32[1024]{0:T(1024)S(1)} %pad_clamp_fusion), kind=kCustom, calls=%fused_computation.1 | custom fusion | bytes 524544 | tf_op jit(solution)/shard_map/jit(_take)/gather | solution.py:89
  42.5 0.7 pad_maximum_fusion.2
  43.2 0.7 fusion.179
  44.5 0.7 copy.106
  45.2 0.6 fusion.34
  45.8 0.6 fusion.38
  46.4 0.6 fusion.3
  47.1 0.9 %multiply_add_fusion = (f32[4,16,32,64]{3,1,2,0:T(8,128)S(1)}, f32[4,16,32,64]{3,1,2,0:T(8,128)S(1)}) fusion(f32[4,16,32,64]{3,1,2,0:T(8,128)S(1)} %fusion.3, f32[16,32]{0,1:T(8,128)S(1)} %get-tuple-element.22, f32[16,32]{0,1:T(8,128)S(1)} %get-tuple-element.23, f32[4,32,64,16]{2,3,1,0:T(8,128)S(1)} %fusion.34, bf16[4,16,32,64]{3,2,1,0:T(8,128)(2,1)S(1)} %bitcast.155), kind=kOutput, calls=%fused_computation.22 | convolution fusion | flops 26087168 | bytes 2363392 | tf_op jit(solution)/shard_map/ka,sabe->skbe/dot_general | solution.py:55
  48.0 1.4 %fusion.12 = f32[4,16,64,32]{2,3,1,0:T(8,128)S(1)} fusion(f32[4,16,32,64]{3,1,2,0:T(8,128)S(1)} %get-tuple-element.4), kind=kOutput, calls=%fused_computation.25 | convolution fusion | flops 50345984 | bytes 1048576 | tf_op jit(solution)/shard_map/qb,skbe->sqke/dot_general | solution.py:65
  49.4 1.4 %fusion.16 = f32[4,16,64,32]{2,3,1,0:T(8,128)S(1)} fusion(f32[4,16,32,64]{3,1,2,0:T(8,128)S(1)} %get-tuple-element.5), kind=kOutput, calls=%fused_computation.29 | convolution fusion | flops 50345984 | bytes 1048576 | tf_op jit(solution)/shard_map/qb,skbe->sqke/dot_general | solution.py:62
  50.8 1.4 %fusion.1 = f32[4,32,16,64]{3,1,2,0:T(8,128)S(1)} fusion(f32[4,16,64,32]{2,3,1,0:T(8,128)S(1)} %fusion.16, f32[4,16,32,64]{3,1,2,0:T(8,128)S(1)} %get-tuple-element.4), kind=kOutput, calls=%fused_computation.5 | convolution fusion | flops 50478080 | bytes 1572864 | tf_op jit(solution)/shard_map/qb,skbe->sqke/dot_general | solution.py:62
  52.2 0.9 %copy-done.1 = f32[4,32,16,64]{3,1,2,0:T(8,128)} copy-done((f32[4,32,16,64]{3,1,2,0:T(8,128)}, f32[4,32,16,64]{3,1,2,0:T(8,128)S(1)}, u32[]{:S(2)}) %copy-start.1) | copy-done | bytes 524312
  53.1 1.4 %fusion = f32[4,32,16,64]{3,1,2,0:T(8,128)S(1)} fusion(f32[4,16,64,32]{2,3,1,0:T(8,128)S(1)} %fusion.12, f32[4,16,32,64]{3,1,2,0:T(8,128)S(1)} %get-tuple-element.5), kind=kOutput, calls=%fused_computation.3 | convolution fusion | flops 50478080 | bytes 1572864 | tf_op jit(solution)/shard_map/qb,skbe->sqke/dot_general | solution.py:65
  54.6 1.0 %copy-done.2 = f32[4,32,16,64]{3,1,2,0:T(8,128)} copy-done((f32[4,32,16,64]{3,1,2,0:T(8,128)}, f32[4,32,16,64]{3,1,2,0:T(8,128)S(1)}, u32[]{:S(2)}) %copy-start.2) | copy-done | bytes 524312
  55.8 0.9 slice-done
  57.2 0.7 slice.80
  58.1 0.9 slice-done.1
  59.5 0.9 slice.89
  60.7 0.9 %fusion.32 = f32[2,32,64,16]{2,3,1,0:T(8,128)S(1)} fusion(f32[2,16,32,64]{3,2,1,0:T(8,128)S(1)} %get-tuple-element.6), kind=kOutput, calls=%fused_computation.60 | convolution fusion | flops 12586496 | bytes 524288 | tf_op jit(solution)/shard_map/ka,sabe->skbe/dot_general | solution.py:52
  61.6 0.9 %fusion.28 = f32[2,32,64,16]{2,3,1,0:T(8,128)S(1)} fusion(f32[2,16,32,64]{3,2,1,0:T(8,128)S(1)} %get-tuple-element.7), kind=kOutput, calls=%fused_computation.56 | convolution fusion | flops 12586496 | bytes 524288 | tf_op jit(solution)/shard_map/ka,sabe->skbe/dot_general | solution.py:55
  62.5 0.9 %fusion.7 = f32[2,16,32,64]{3,1,2,0:T(8,128)S(1)} fusion(f32[2,32,64,16]{2,3,1,0:T(8,128)S(1)} %fusion.32, f32[2,16,32,64]{3,2,1,0:T(8,128)S(1)} %get-tuple-element.7), kind=kOutput, calls=%fused_computation.17 | convolution fusion | flops 12652032 | bytes 786432 | tf_op jit(solution)/shard_map/ka,sabe->skbe/dot_general | solution.py:52
  63.4 1.1 %multiply_subtract_fusion.1 = (f32[2,16,32,64]{3,1,2,0:T(8,128)S(1)}, f32[2,16,32,64]{3,1,2,0:T(8,128)S(1)}) fusion(f32[2,16,32,64]{3,1,2,0:T(8,128)S(1)} %fusion.7, f32[16,32]{0,1:T(8,128)S(1)} %get-tuple-element.23, f32[16,32]{0,1:T(8,128)S(1)} %fusion.89, f32[2,32,64,16]{2,3,1,0:T(8,128)S(1)} %fusion.28, f32[2,16,32,64]{3,2,1,0:T(8,128)S(1)} %get-tuple-element.6), kind=kOutput, calls=%fused_computation.47 | convolution fusion | flops 13045248 | bytes 1314816 | tf_op jit(solution)/shard_map/ka,sabe->skbe/dot_general | solution.py:55
  64.5 0.8 fusion.22
  65.2 0.8 fusion.26
  66.0 0.8 fusion.10
  66.8 0.8 fusion.11
  68.2 0.9 %reshape.179 = bf16[8,2,4096]{2,1,0:T(2,128)(2,1)} reshape(bf16[512,2,64]{2,1,0:T(2,128)(2,1)S(1)} %bitcast.176) | data formatting | bytes 262144
  69.1 3.4 %all-to-all-start.3 = ((bf16[8,2,4096]{2,1,0:T(2,128)(2,1)}), bf16[8,2,4096]{2,1,0:T(2,128)(2,1)S(1)}, u32[]{:S(2)}, u32[]{:S(2)}) async-start(bf16[8,2,4096]{2,1,0:T(2,128)(2,1)} %reshape.179), calls=%async_computation.3 | async-start | bytes 262144 | tf_op jit(solution)/shard_map/all_to_all | solution.py:104
  72.8 0.9 %reshape.177 = bf16[8,2,4096]{2,1,0:T(2,128)(2,1)} reshape(bf16[512,2,64]{2,1,0:T(2,128)(2,1)S(1)} %bitcast.177) | data formatting | bytes 262144
  73.7 4.3 %all-to-all-done.3 = bf16[8,2,4096]{2,1,0:T(2,128)(2,1)S(1)} async-done(((bf16[8,2,4096]{2,1,0:T(2,128)(2,1)}), bf16[8,2,4096]{2,1,0:T(2,128)(2,1)S(1)}, u32[]{:S(2)}, u32[]{:S(2)}) %all-to-all-start.3) | async-done | bytes 131104 | tf_op jit(solution)/shard_map/all_to_all | solution.py:104
  78.0 3.4 %all-to-all-start.2 = ((bf16[8,2,4096]{2,1,0:T(2,128)(2,1)}), bf16[8,2,4096]{2,1,0:T(2,128)(2,1)S(1)}, u32[]{:S(2)}, u32[]{:S(2)}) async-start(bf16[8,2,4096]{2,1,0:T(2,128)(2,1)} %reshape.177), calls=%async_computation.2 | async-start | bytes 262144 | tf_op jit(solution)/shard_map/all_to_all | solution.py:103
  81.7 0.9 all_to_all.61
  82.6 4.2 %all-to-all-done.2 = bf16[8,2,4096]{2,1,0:T(2,128)(2,1)S(1)} async-done(((bf16[8,2,4096]{2,1,0:T(2,128)(2,1)}), bf16[8,2,4096]{2,1,0:T(2,128)(2,1)S(1)}, u32[]{:S(2)}, u32[]{:S(2)}) %all-to-all-start.2) | async-done | bytes 131104 | tf_op jit(solution)/shard_map/all_to_all | solution.py:103
  87.2 0.9 all_to_all.57
  (61 shorter events, 8.0 us)
Async XLA Ops:
  0.6 7.3 %copy-start = (s32[1,8,4,32]{3,2,1,0:T(4,128)S(1)}, s32[1,8,4,32]{3,2,1,0:T(4,128)}, u32[]{:S(2)}) copy-start(s32[1,8,4,32]{3,2,1,0:T(4,128)} %param.6) | copy-start | bytes 12292
  2.6 6.3 %copy-start.3 = (bf16[2,64,512]{2,1,0:T(8,128)(2,1)S(1)}, bf16[2,64,512]{2,1,0:T(8,128)(2,1)}, u32[]{:S(2)}) copy-start(bf16[2,64,512]{2,1,0:T(8,128)(2,1)} %param.5) | copy-start | bytes 393220
  2.6 10.8 %all-to-all-start = ((bf16[8,2,4096]{2,1,0:T(2,128)(2,1)}), bf16[8,2,4096]{2,1,0:T(2,128)(2,1)S(1)}, u32[]{:S(2)}, u32[]{:S(2)}) async-start(bf16[8,2,4096]{2,1,0:T(2,128)(2,1)} %reshape.175), calls=%async_computation | async-start | bytes 262144 | tf_op jit(solution)/shard_map/all_to_all | solution.py:81
  13.5 8.8 %all-to-all-start.1 = ((bf16[8,2,4096]{2,1,0:T(2,128)(2,1)}), bf16[8,2,4096]{2,1,0:T(2,128)(2,1)S(1)}, u32[]{:S(2)}, u32[]{:S(2)}) async-start(bf16[8,2,4096]{2,1,0:T(2,128)(2,1)} %reshape.173), calls=%async_computation.1 | async-start | bytes 262144 | tf_op jit(solution)/shard_map/all_to_all | solution.py:82
  26.2 14.7 %collective-permute-start.2 = (bf16[2,2,512,32]{2,1,0,3:T(2,128)(2,1)S(1)}, bf16[2,2,512,32]{2,1,0,3:T(2,128)(2,1)S(1)}, u32[]{:S(2)}, u32[]{:S(2)}) collective-permute-start(bf16[2,2,512,32]{2,1,0,3:T(2,128)(2,1)S(1)} %get-tuple-element.18), channel_id=1, source_target_pairs={{0,3},{1,2},{2,1},{3,0},{4,7},{5,6},{6,5},{7,4},{8,11},{9,10},{10,... | collective-permute-start | bytes 393224 | tf_op jit(solution)/shard_map/ppermute | solution.py:20
  29.9 10.9 %collective-permute-start.1 = (bf16[2,2,512,32]{2,1,0,3:T(2,128)(2,1)S(1)}, bf16[2,2,512,32]{2,1,0,3:T(2,128)(2,1)S(1)}, u32[]{:S(2)}, u32[]{:S(2)}) collective-permute-start(bf16[2,2,512,32]{2,1,0,3:T(2,128)(2,1)S(1)} %get-tuple-element.19), channel_id=1, source_target_pairs={{0,2},{1,3},{2,0},{3,1},{4,6},{5,7},{6,4},{7,5},{8,10},{9,11},{10,... | collective-permute-start | bytes 393224 | tf_op jit(solution)/shard_map/ppermute | solution.py:20
  29.9 8.2 %collective-permute-start = (bf16[2,2,512,32]{2,1,0,3:T(2,128)(2,1)S(1)}, bf16[2,2,512,32]{2,1,0,3:T(2,128)(2,1)S(1)}, u32[]{:S(2)}, u32[]{:S(2)}) collective-permute-start(bf16[2,2,512,32]{2,1,0,3:T(2,128)(2,1)S(1)} %get-tuple-element.20), channel_id=1, source_target_pairs={{0,1},{1,0},{2,3},{3,2},{4,5},{5,4},{6,7},{7,6},{8,9},{9,8},{10,11... | collective-permute-start | bytes 393224 | tf_op jit(solution)/shard_map/ppermute | solution.py:20
  52.2 1.0 %copy-start.1 = (f32[4,32,16,64]{3,1,2,0:T(8,128)}, f32[4,32,16,64]{3,1,2,0:T(8,128)S(1)}, u32[]{:S(2)}) copy-start(f32[4,32,16,64]{3,1,2,0:T(8,128)S(1)} %fusion.1) | copy-start | bytes 1572868
  54.5 1.0 %copy-start.2 = (f32[4,32,16,64]{3,1,2,0:T(8,128)}, f32[4,32,16,64]{3,1,2,0:T(8,128)S(1)}, u32[]{:S(2)}) copy-start(f32[4,32,16,64]{3,1,2,0:T(8,128)S(1)} %fusion) | copy-start | bytes 1572868
  55.6 1.0 %slice-start = ((f32[4,32,16,64]{3,1,2,0:T(8,128)}), f32[2,32,16,64]{3,1,2,0:T(8,128)S(1)}, s32[]{:S(2)}) async-start(f32[4,32,16,64]{3,1,2,0:T(8,128)} %copy-done.1), calls=%async_computation.4 | async-start | bytes 1048576 | tf_op jit(solution)/shard_map/slice | solution.py:92
  57.9 1.0 %slice-start.1 = ((f32[4,32,16,64]{3,1,2,0:T(8,128)}), f32[2,32,16,64]{3,1,2,0:T(8,128)S(1)}, s32[]{:S(2)}) async-start(f32[4,32,16,64]{3,1,2,0:T(8,128)} %copy-done.2), calls=%async_computation.5 | async-start | bytes 1048576 | tf_op jit(solution)/shard_map/slice | solution.py:93
  69.1 8.8 %all-to-all-start.3 = ((bf16[8,2,4096]{2,1,0:T(2,128)(2,1)}), bf16[8,2,4096]{2,1,0:T(2,128)(2,1)S(1)}, u32[]{:S(2)}, u32[]{:S(2)}) async-start(bf16[8,2,4096]{2,1,0:T(2,128)(2,1)} %reshape.179), calls=%async_computation.3 | async-start | bytes 262144 | tf_op jit(solution)/shard_map/all_to_all | solution.py:104
  78.0 8.8 %all-to-all-start.2 = ((bf16[8,2,4096]{2,1,0:T(2,128)(2,1)}), bf16[8,2,4096]{2,1,0:T(2,128)(2,1)S(1)}, u32[]{:S(2)}, u32[]{:S(2)}) async-start(bf16[8,2,4096]{2,1,0:T(2,128)(2,1)} %reshape.177), calls=%async_computation.2 | async-start | bytes 262144 | tf_op jit(solution)/shard_map/all_to_all | solution.py:103
